TPU v7x, 256 devices: a whole 4x4x8 slice. The times are simulated.
256 devices in a mesh: space: 32 (over z_lo, y, core), dom: 8 (over z_hi, x).
Axes of the slice: x: 4, y: 4, z: 8 (z_hi: 2, z_lo: 4; z = z_hi * 4 + z_lo), core: 2. Of those that a mesh axis runs over, the one named last changes fastest.
Arguments:
- water_depth: float32 [16, 32, 256, 512], P('dom', 'space'), may hold values from 0 to 1.5
- infiltrated: float32 [16, 32, 256, 512], P('dom', 'space'), may hold values from 0.2 to 2
- terrain: float32 [32, 256, 512], P('space'), may hold values from -3 to 3
- land_mask: int32 [32, 256, 512], P('space'), may hold values from 0 to 1
- forcing: bfloat16 [2, 2, 32, 256, 512], P(None, None, 'space', 'dom'), may hold values from 0.049804688 to 1.5
- observed: bfloat16 [2, 32, 256, 512], P(None, 'space'), may hold values from 0 to 3.6
- conductivity: float32 [16], replicated, may hold values from 0.05 to 0.6
- suction: float32 [16], replicated, may hold values from 0.1 to 2
- manning: float32 [16], replicated, may hold values from 0.5 to 2
- assignment: int32 [16], P('dom'), may hold values from 0 to 15, each once
- ancestors: int32 [16], P('dom'), may hold values from 0 to 15, as said below
- prior_weight: float32 [16], P('dom'), may hold values from 0.01 to 1
Outputs:
- final_depth: float32 [16, 32, 256, 512], P('dom', 'space')
- final_infiltrated: float32 [16, 32, 256, 512], P('dom', 'space')
- weights: float32 [16], P('dom')
Inputs may be any that keep to these rules, and one draw needn't show every extreme that they name: `ancestors`: the ancestor of slot s is a slot of its own group, 2 * (s // 2) to 2 * (s // 2) + 1; slot 0's ancestor is 0 and the last slot's is itself.
All inputs are finite; a program needn't handle non-finite values.
Results may differ from a plain program's by a relative error of at most 0.0003.
Values may be sent and summed in bfloat16 or wider, within the bound.
No kernel may reach another device: no remote copies, remote signals or barrier semaphores. Data moves between devices by JAX's collectives and lax.ppermute only.
A program may use at most 64 MiB of HBM per device.

v0:
```python
import jax
import jax.numpy as jnp
from jax import lax
from jax.sharding import PartitionSpec as P

TX = 4
SUB = 6
HOURS = 2
time_step = 0.01
slope_floor = 0.1
sharpness = 20.0


def passed_along(block, axis, distance):
    devices = range(lax.axis_size(axis))
    route = [(i - distance, i) for i in devices if i - distance in devices]
    return lax.ppermute(block, axis, route)


def passed_along_2(array, axis, by):
    devices = lax.axis_size(axis)
    return lax.ppermute(array, axis, [(i, (i + by) % devices) for i in range(devices)])


def shift_rows(edge, offset):
    return passed_along(edge, "space", offset)


def shift_cols(edge, offset):
    return passed_along_2(edge, "space", offset)


def from_west(edge, column_tile, shifter):
    near = shifter(edge, 1)
    far = shifter(edge, -(TX - 1))
    return jnp.where(column_tile == 0, far, near)


def from_east(edge, column_tile, shifter):
    near = shifter(edge, -1)
    far = shifter(edge, TX - 1)
    return jnp.where(column_tile == TX - 1, far, near)


def with_rims(field, column_tile):
    north = shift_rows(field[..., -1, :], TX)
    south = shift_rows(field[..., 0, :], -TX)
    west = from_west(field[..., :, -1], column_tile, shift_cols)
    east = from_east(field[..., :, 0], column_tile, shift_cols)
    tall = jnp.concatenate([north[..., None, :], field, south[..., None, :]], axis=-2)
    corner = jnp.zeros(field.shape[:-2] + (1,), field.dtype)
    west_col = jnp.concatenate([corner, west, corner], axis=-1)[..., None]
    east_col = jnp.concatenate([corner, east, corner], axis=-1)[..., None]
    return jnp.concatenate([west_col, tall, east_col], axis=-1)


def face_flux(depth_a, depth_b, level_a, level_b, rough):
    slope = level_b - level_a
    mean_depth = 0.5 * (depth_a + depth_b)
    return (
        -jnp.power(mean_depth, 5.0 / 3.0) * slope / (rough * jnp.sqrt(jnp.abs(slope) + slope_floor))
    )


def flow_step(depth_now, soak_now, padded, level, net_rain, land, conduct, suction_p, rough):
    flux_cols = face_flux(
        padded[:, 1:-1, :-1], padded[:, 1:-1, 1:], level[:, 1:-1, :-1], level[:, 1:-1, 1:], rough
    )
    flux_rows = face_flux(
        padded[:, :-1, 1:-1], padded[:, 1:, 1:-1], level[:, :-1, 1:-1], level[:, 1:, 1:-1], rough
    )
    outflow = (
        flux_cols[:, :, 1:] - flux_cols[:, :, :-1] + flux_rows[:, 1:, :] - flux_rows[:, :-1, :]
    )
    ponded = jnp.maximum(depth_now - time_step * outflow + time_step * net_rain, 0.0)
    capacity = conduct * (1.0 + suction_p / soak_now)
    intake = jnp.minimum(time_step * capacity, ponded)
    return ((ponded - intake) * land, soak_now + intake * land)


def local(
    water_depth,
    infiltrated,
    terrain,
    land_mask,
    forcing,
    observed,
    conductivity,
    suction,
    manning,
    assignment,
    ancestors,
    prior_weight,
):
    per_group = water_depth.shape[0]
    first_slot = lax.axis_index("dom") * per_group
    local_slot = ancestors - first_slot
    water = jnp.take(water_depth[:, 0], local_slot, axis=0)
    soaked = jnp.take(infiltrated[:, 0], local_slot, axis=0)
    owners = jnp.take(assignment, local_slot)
    every_slot = jnp.arange(conductivity.shape[0], dtype=jnp.int32)
    picker = owners[:, None] == every_slot[None, :]

    def lookup(table):
        return jnp.sum(jnp.where(picker, table[None, :], 0.0), axis=1)[:, None, None]

    conduct = lookup(conductivity)
    suction_p = lookup(suction)
    rough = lookup(manning)
    group_mean = jnp.mean(prior_weight)
    column_tile = lax.axis_index("space") % TX
    land = land_mask[0].astype(jnp.float32)
    ground = with_rims(terrain[0], column_tile)
    window_forcing = lax.all_gather(forcing, "dom", axis=3, tiled=True)
    misfit = jnp.zeros((per_group,), jnp.float32)
    for hour in range(HOURS):
        hour_forcing = window_forcing[hour]
        net_rain = hour_forcing[0, 0].astype(jnp.float32) - hour_forcing[1, 0].astype(jnp.float32)

        def advance(index, carry):
            depth_now, soak_now = carry
            padded = with_rims(depth_now, column_tile)
            level = padded + ground[None]
            return flow_step(
                depth_now, soak_now, padded, level, net_rain, land, conduct, suction_p, rough
            )

        water, soaked = lax.fori_loop(0, SUB, advance, (water, soaked))
        gap = water - observed[hour, 0].astype(jnp.float32)
        square = gap * gap
        misfit = misfit + jnp.sum(land * square / (1.0 + square), axis=(1, 2))
    cells = HOURS * jnp.sum(land)
    summed = lax.psum((misfit, cells), "space")
    raw = group_mean * jnp.exp(-sharpness * summed[0] / summed[1])
    total = lax.psum(jnp.sum(raw), "dom")
    weights = raw / total
    return (water[:, None], soaked[:, None], weights)


def solution(mesh):
    return jax.shard_map(
        local,
        mesh=mesh,
        in_specs=(
            P("dom", "space", None, None),
            P("dom", "space", None, None),
            P("space", None, None),
            P("space", None, None),
            P(None, None, "space", "dom", None),
            P(None, "space", None, None),
            P(),
            P(),
            P(),
            P("dom"),
            P("dom"),
            P("dom"),
        ),
        out_specs=(P("dom", "space", None, None), P("dom", "space", None, None), P("dom")),
        check_vma=False,
    )
```

profile of v0, /device:TPU:0, one launch (start us, length us, event | category | flops | bytes accessed | tf_op | source)
XLA Modules:
  0.0 788.4 jit_solution(13854615685803920261)
XLA Ops:
  53.1 27.6 %all-gather.2.cloned.1.call-done = bf16[2,2,1,256,512]{4,1,2,0,3:T(2,128)(2,1)} async-done(((bf16[2,2,1,32,512]{4,1,2,0,3:T(2,128)(2,1)}), bf16[2,2,1,256,512]{4,1,2,0,3:T(2,128)(2,1)}) %all-gather.2.cloned.1.call-update) | async-done | bytes 1048592 | tf_op jit(solution)/shard_map/all_gather | solution.py:114
  87.6 284.1 %while.28 = (s32[]{:T(128)}, f32[2,256,512]{1,0,2:T(2,128)S(1)}, f32[2,256,512]{1,0,2:T(2,128)}, pred[]{:T(512)}, pred[]{:T(512)}, /*index=5*/f32[258,514]{0,1:T...) while((s32[]{:T(128)}, f32[2,256,512]{1,0,2:T(2,128)S(1)}, ...), condition=%wide.region_4.6_spmd, body=%wide.region_3.5_spmd.sunk | while | flops 12489274 | bytes 36930208 | solution.py:128
  114.2 7.3 multiply_divide_fusion.4
  121.5 8.1 %fusion.47 = f32[2,257,512]{1,0,2:T(2,128)S(1)} fusion(f32[2,256,512]{1,0,2:T(2,128)S(1)} %get-tuple-element.585, f32[2,1,512]{1,0,2:T(2,128)S(1)} %copy.141, f32[2,1,512]{1,0,2:T(2,128)S(1)} %copy-done.5, f32[2,258,514]{1,0,2:T(2,128)S(1)} %maximum_add_fusion.6, f32[2]{0:T(128)S(1)} %bitcast.100), kind=kLoop, calls=%fused_computation.10.clone.1 | loop fusion | flops 2894848 | bytes 4214792 | tf_op jit(solution)/shard_map/while/body/eval_jaxpr/div | solution.py:61
  161.4 7.3 multiply_divide_fusion.4
  168.7 8.1 %fusion.47 = f32[2,257,512]{1,0,2:T(2,128)S(1)} fusion(f32[2,256,512]{1,0,2:T(2,128)S(1)} %get-tuple-element.585, f32[2,1,512]{1,0,2:T(2,128)S(1)} %copy.141, f32[2,1,512]{1,0,2:T(2,128)S(1)} %copy-done.5, f32[2,258,514]{1,0,2:T(2,128)S(1)} %maximum_add_fusion.6, f32[2]{0:T(128)S(1)} %bitcast.100), kind=kLoop, calls=%fused_computation.10.clone.1 | loop fusion | flops 2894848 | bytes 4214792 | tf_op jit(solution)/shard_map/while/body/eval_jaxpr/div | solution.py:61
  208.6 7.3 multiply_divide_fusion.4
  215.9 8.1 %fusion.47 = f32[2,257,512]{1,0,2:T(2,128)S(1)} fusion(f32[2,256,512]{1,0,2:T(2,128)S(1)} %get-tuple-element.585, f32[2,1,512]{1,0,2:T(2,128)S(1)} %copy.141, f32[2,1,512]{1,0,2:T(2,128)S(1)} %copy-done.5, f32[2,258,514]{1,0,2:T(2,128)S(1)} %maximum_add_fusion.6, f32[2]{0:T(128)S(1)} %bitcast.100), kind=kLoop, calls=%fused_computation.10.clone.1 | loop fusion | flops 2894848 | bytes 4214792 | tf_op jit(solution)/shard_map/while/body/eval_jaxpr/div | solution.py:61
  255.8 7.3 multiply_divide_fusion.4
  263.1 8.1 %fusion.47 = f32[2,257,512]{1,0,2:T(2,128)S(1)} fusion(f32[2,256,512]{1,0,2:T(2,128)S(1)} %get-tuple-element.585, f32[2,1,512]{1,0,2:T(2,128)S(1)} %copy.141, f32[2,1,512]{1,0,2:T(2,128)S(1)} %copy-done.5, f32[2,258,514]{1,0,2:T(2,128)S(1)} %maximum_add_fusion.6, f32[2]{0:T(128)S(1)} %bitcast.100), kind=kLoop, calls=%fused_computation.10.clone.1 | loop fusion | flops 2894848 | bytes 4214792 | tf_op jit(solution)/shard_map/while/body/eval_jaxpr/div | solution.py:61
  303.0 7.3 multiply_divide_fusion.4
  310.3 8.1 %fusion.47 = f32[2,257,512]{1,0,2:T(2,128)S(1)} fusion(f32[2,256,512]{1,0,2:T(2,128)S(1)} %get-tuple-element.585, f32[2,1,512]{1,0,2:T(2,128)S(1)} %copy.141, f32[2,1,512]{1,0,2:T(2,128)S(1)} %copy-done.5, f32[2,258,514]{1,0,2:T(2,128)S(1)} %maximum_add_fusion.6, f32[2]{0:T(128)S(1)} %bitcast.100), kind=kLoop, calls=%fused_computation.10.clone.1 | loop fusion | flops 2894848 | bytes 4214792 | tf_op jit(solution)/shard_map/while/body/eval_jaxpr/div | solution.py:61
  323.9 6.9 collective-permute-start.2
  350.6 7.3 multiply_divide_fusion.4
  357.9 8.1 %fusion.47 = f32[2,257,512]{1,0,2:T(2,128)S(1)} fusion(f32[2,256,512]{1,0,2:T(2,128)S(1)} %get-tuple-element.585, f32[2,1,512]{1,0,2:T(2,128)S(1)} %copy.141, f32[2,1,512]{1,0,2:T(2,128)S(1)} %copy-done.5, f32[2,258,514]{1,0,2:T(2,128)S(1)} %maximum_add_fusion.6, f32[2]{0:T(128)S(1)} %bitcast.100), kind=kLoop, calls=%fused_computation.10.clone.1 | loop fusion | flops 2894848 | bytes 4214792 | tf_op jit(solution)/shard_map/while/body/eval_jaxpr/div | solution.py:61
  372.9 298.5 %while.29 = (s32[]{:T(128)}, f32[2,256,512]{1,0,2:T(2,128)S(1)}, f32[2,256,512]{1,0,2:T(2,128)}, pred[]{:T(512)}, pred[]{:T(512)}, /*index=5*/f32[258,514]{0,1:T...) while((s32[]{:T(128)}, f32[2,256,512]{1,0,2:T(2,128)S(1)}, ...), condition=%wide.region_6.8_spmd, body=%wide.region_5.7_spmd.sunk | while | flops 12489274 | bytes 39043804 | solution.py:128
  373.0 7.5 collective-permute-start.8
  402.3 7.3 multiply_divide_fusion.5
  409.6 8.1 %fusion.50 = f32[2,257,512]{1,0,2:T(2,128)S(1)} fusion(f32[2,256,512]{1,0,2:T(2,128)S(1)} %get-tuple-element.624, f32[2,1,512]{1,0,2:T(2,128)S(1)} %copy-done.4, f32[2,1,512]{1,0,2:T(2,128)S(1)} %copy-done.6, f32[2,258,514]{1,0,2:T(2,128)S(1)} %maximum_add_fusion.7, f32[2]{0:T(128)S(1)} %bitcast.102), kind=kLoop, calls=%fused_computation.50.clone.1 | loop fusion | flops 2894848 | bytes 4214792 | tf_op jit(solution)/shard_map/while/body/eval_jaxpr/div | solution.py:61
  423.3 7.2 collective-permute-start.8
  452.3 7.3 multiply_divide_fusion.5
  459.6 8.1 %fusion.50 = f32[2,257,512]{1,0,2:T(2,128)S(1)} fusion(f32[2,256,512]{1,0,2:T(2,128)S(1)} %get-tuple-element.624, f32[2,1,512]{1,0,2:T(2,128)S(1)} %copy-done.4, f32[2,1,512]{1,0,2:T(2,128)S(1)} %copy-done.6, f32[2,258,514]{1,0,2:T(2,128)S(1)} %maximum_add_fusion.7, f32[2]{0:T(128)S(1)} %bitcast.102), kind=kLoop, calls=%fused_computation.50.clone.1 | loop fusion | flops 2894848 | bytes 4214792 | tf_op jit(solution)/shard_map/while/body/eval_jaxpr/div | solution.py:61
  501.8 7.3 multiply_divide_fusion.5
  509.1 8.1 %fusion.50 = f32[2,257,512]{1,0,2:T(2,128)S(1)} fusion(f32[2,256,512]{1,0,2:T(2,128)S(1)} %get-tuple-element.624, f32[2,1,512]{1,0,2:T(2,128)S(1)} %copy-done.4, f32[2,1,512]{1,0,2:T(2,128)S(1)} %copy-done.6, f32[2,258,514]{1,0,2:T(2,128)S(1)} %maximum_add_fusion.7, f32[2]{0:T(128)S(1)} %bitcast.102), kind=kLoop, calls=%fused_computation.50.clone.1 | loop fusion | flops 2894848 | bytes 4214792 | tf_op jit(solution)/shard_map/while/body/eval_jaxpr/div | solution.py:61
  551.4 7.3 multiply_divide_fusion.5
  558.7 8.1 %fusion.50 = f32[2,257,512]{1,0,2:T(2,128)S(1)} fusion(f32[2,256,512]{1,0,2:T(2,128)S(1)} %get-tuple-element.624, f32[2,1,512]{1,0,2:T(2,128)S(1)} %copy-done.4, f32[2,1,512]{1,0,2:T(2,128)S(1)} %copy-done.6, f32[2,258,514]{1,0,2:T(2,128)S(1)} %maximum_add_fusion.7, f32[2]{0:T(128)S(1)} %bitcast.102), kind=kLoop, calls=%fused_computation.50.clone.1 | loop fusion | flops 2894848 | bytes 4214792 | tf_op jit(solution)/shard_map/while/body/eval_jaxpr/div | solution.py:61
  600.9 7.3 multiply_divide_fusion.5
  608.2 8.1 %fusion.50 = f32[2,257,512]{1,0,2:T(2,128)S(1)} fusion(f32[2,256,512]{1,0,2:T(2,128)S(1)} %get-tuple-element.624, f32[2,1,512]{1,0,2:T(2,128)S(1)} %copy-done.4, f32[2,1,512]{1,0,2:T(2,128)S(1)} %copy-done.6, f32[2,258,514]{1,0,2:T(2,128)S(1)} %maximum_add_fusion.7, f32[2]{0:T(128)S(1)} %bitcast.102), kind=kLoop, calls=%fused_computation.50.clone.1 | loop fusion | flops 2894848 | bytes 4214792 | tf_op jit(solution)/shard_map/while/body/eval_jaxpr/div | solution.py:61
  650.5 7.3 multiply_divide_fusion.5
  657.8 8.1 %fusion.50 = f32[2,257,512]{1,0,2:T(2,128)S(1)} fusion(f32[2,256,512]{1,0,2:T(2,128)S(1)} %get-tuple-element.624, f32[2,1,512]{1,0,2:T(2,128)S(1)} %copy-done.4, f32[2,1,512]{1,0,2:T(2,128)S(1)} %copy-done.6, f32[2,258,514]{1,0,2:T(2,128)S(1)} %maximum_add_fusion.7, f32[2]{0:T(128)S(1)} %bitcast.102), kind=kLoop, calls=%fused_computation.50.clone.1 | loop fusion | flops 2894848 | bytes 4214792 | tf_op jit(solution)/shard_map/while/body/eval_jaxpr/div | solution.py:61
  678.7 72.3 %all-reduce = (f32[2]{0:T(128)S(1)}, f32[]{:T(128)}) all-reduce(f32[2]{0:T(128)S(1)} %add.160, f32[]{:T(128)S(6)} %mul.249), channel_id=1, replica_groups=mesh['space'=32,'dom'=8] {'space'}, use_global_device_ids=true, to_apply=%region_10.12 | all-reduce | flops 3 | bytes 24 | tf_op jit(solution)/shard_map/psum | solution.py:133
  752.4 27.7 %psum.23 = f32[]{:T(128)} all-reduce(f32[]{:T(128)} %get-tuple-element.375), channel_id=1, replica_groups=mesh['space'=32,'dom'=8] {'dom'}, use_global_device_ids=true, to_apply=%region_14.16 | all-reduce | flops 1 | bytes 8 | tf_op jit(solution)/shard_map/psum | solution.py:135
  (503 shorter events, 436.2 us)
Async XLA Ops:
  7.2 73.5 %all-gather.2.cloned.1.call-start = ((), (), s32[]{:S(2)}) async-start(), calls=%async_computation | async-start | bytes 1179648 | tf_op jit(solution)/shard_map/all_gather | solution.py:114
  8.6 33.9 %collective-permute-start.17 = (f32[256]{0:T(256)S(1)}, f32[256]{0:T(256)S(1)}, u32[]{:S(2)}, u32[]{:S(2)}) collective-permute-start(f32[256]{0:T(256)S(1)} %bitcast.123), channel_id=1, source_target_pairs={{0,248},{8,0},{16,8},{24,16},{32,24},{40,32},{48,40},{56,48},{64,5... | collective-permute-start | bytes 3080 | tf_op jit(solution)/shard_map/ppermute | solution.py:22
  13.5 35.1 %collective-permute-start.16 = (f32[256]{0:T(256)S(1)}, f32[256]{0:T(256)S(1)}, u32[]{:S(2)}, u32[]{:S(2)}) collective-permute-start(f32[256]{0:T(256)S(1)} %bitcast.124), channel_id=1, source_target_pairs={{0,24},{8,32},{16,40},{24,48},{32,56},{40,64},{48,72},{56,80},{64,... | collective-permute-start | bytes 3080 | tf_op jit(solution)/shard_map/ppermute | solution.py:22
  13.5 35.2 %collective-permute-start.13 = (f32[256]{0:T(256)S(1)}, f32[256]{0:T(256)S(1)}, u32[]{:S(2)}, u32[]{:S(2)}) collective-permute-start(f32[256]{0:T(256)S(1)} %bitcast.121), channel_id=1, source_target_pairs={{0,8},{8,16},{16,24},{24,32},{32,40},{40,48},{48,56},{56,64},{64,7... | collective-permute-start | bytes 3080 | tf_op jit(solution)/shard_map/ppermute | solution.py:22
  13.5 35.2 %collective-permute-start.12 = (f32[256]{0:T(256)S(1)}, f32[256]{0:T(256)S(1)}, u32[]{:S(2)}, u32[]{:S(2)}) collective-permute-start(f32[256]{0:T(256)S(1)} %bitcast.122), channel_id=1, source_target_pairs={{0,232},{8,240},{16,248},{24,0},{32,8},{40,16},{48,24},{56,32},{64... | collective-permute-start | bytes 3080 | tf_op jit(solution)/shard_map/ppermute | solution.py:22
  87.9 18.8 %collective-permute-start.2 = (f32[2,256]{1,0:T(2,128)S(1)}, f32[2,256]{1,0:T(2,128)S(1)}, u32[]{:S(2)}, u32[]{:S(2)}) collective-permute-start(f32[2,256]{1,0:T(2,128)S(1)} %get-tuple-element.544), channel_id=1, source_target_pairs={{0,232},{8,240},{16,248},{24,0},{32,8},{40,16},{48,24},{56,32},{64... | collective-permute-start | bytes 6152 | tf_op jit(solution)/shard_map/while/body/eval_jaxpr/ppermute | solution.py:22
  91.1 15.7 %collective-permute-start.5 = (f32[2,256]{1,0:T(2,128)S(1)}, f32[2,256]{1,0:T(2,128)S(1)}, u32[]{:S(2)}, u32[]{:S(2)}) collective-permute-start(f32[2,256]{1,0:T(2,128)S(1)} %get-tuple-element.545), channel_id=1, source_target_pairs={{0,248},{8,0},{16,8},{24,16},{32,24},{40,32},{48,40},{56,48},{64,5... | collective-permute-start | bytes 6152 | tf_op jit(solution)/shard_map/while/body/eval_jaxpr/ppermute | solution.py:22
  135.1 18.8 %collective-permute-start.2 = (f32[2,256]{1,0:T(2,128)S(1)}, f32[2,256]{1,0:T(2,128)S(1)}, u32[]{:S(2)}, u32[]{:S(2)}) collective-permute-start(f32[2,256]{1,0:T(2,128)S(1)} %get-tuple-element.544), channel_id=1, source_target_pairs={{0,232},{8,240},{16,248},{24,0},{32,8},{40,16},{48,24},{56,32},{64... | collective-permute-start | bytes 6152 | tf_op jit(solution)/shard_map/while/body/eval_jaxpr/ppermute | solution.py:22
  138.9 15.1 %collective-permute-start.5 = (f32[2,256]{1,0:T(2,128)S(1)}, f32[2,256]{1,0:T(2,128)S(1)}, u32[]{:S(2)}, u32[]{:S(2)}) collective-permute-start(f32[2,256]{1,0:T(2,128)S(1)} %get-tuple-element.545), channel_id=1, source_target_pairs={{0,248},{8,0},{16,8},{24,16},{32,24},{40,32},{48,40},{56,48},{64,5... | collective-permute-start | bytes 6152 | tf_op jit(solution)/shard_map/while/body/eval_jaxpr/ppermute | solution.py:22
  182.3 18.8 %collective-permute-start.2 = (f32[2,256]{1,0:T(2,128)S(1)}, f32[2,256]{1,0:T(2,128)S(1)}, u32[]{:S(2)}, u32[]{:S(2)}) collective-permute-start(f32[2,256]{1,0:T(2,128)S(1)} %get-tuple-element.544), channel_id=1, source_target_pairs={{0,232},{8,240},{16,248},{24,0},{32,8},{40,16},{48,24},{56,32},{64... | collective-permute-start | bytes 6152 | tf_op jit(solution)/shard_map/while/body/eval_jaxpr/ppermute | solution.py:22
  187.5 13.7 %collective-permute-start.5 = (f32[2,256]{1,0:T(2,128)S(1)}, f32[2,256]{1,0:T(2,128)S(1)}, u32[]{:S(2)}, u32[]{:S(2)}) collective-permute-start(f32[2,256]{1,0:T(2,128)S(1)} %get-tuple-element.545), channel_id=1, source_target_pairs={{0,248},{8,0},{16,8},{24,16},{32,24},{40,32},{48,40},{56,48},{64,5... | collective-permute-start | bytes 6152 | tf_op jit(solution)/shard_map/while/body/eval_jaxpr/ppermute | solution.py:22
  229.5 18.8 %collective-permute-start.2 = (f32[2,256]{1,0:T(2,128)S(1)}, f32[2,256]{1,0:T(2,128)S(1)}, u32[]{:S(2)}, u32[]{:S(2)}) collective-permute-start(f32[2,256]{1,0:T(2,128)S(1)} %get-tuple-element.544), channel_id=1, source_target_pairs={{0,232},{8,240},{16,248},{24,0},{32,8},{40,16},{48,24},{56,32},{64... | collective-permute-start | bytes 6152 | tf_op jit(solution)/shard_map/while/body/eval_jaxpr/ppermute | solution.py:22
  234.9 13.5 %collective-permute-start.5 = (f32[2,256]{1,0:T(2,128)S(1)}, f32[2,256]{1,0:T(2,128)S(1)}, u32[]{:S(2)}, u32[]{:S(2)}) collective-permute-start(f32[2,256]{1,0:T(2,128)S(1)} %get-tuple-element.545), channel_id=1, source_target_pairs={{0,248},{8,0},{16,8},{24,16},{32,24},{40,32},{48,40},{56,48},{64,5... | collective-permute-start | bytes 6152 | tf_op jit(solution)/shard_map/while/body/eval_jaxpr/ppermute | solution.py:22
  276.7 18.9 %collective-permute-start.2 = (f32[2,256]{1,0:T(2,128)S(1)}, f32[2,256]{1,0:T(2,128)S(1)}, u32[]{:S(2)}, u32[]{:S(2)}) collective-permute-start(f32[2,256]{1,0:T(2,128)S(1)} %get-tuple-element.544), channel_id=1, source_target_pairs={{0,232},{8,240},{16,248},{24,0},{32,8},{40,16},{48,24},{56,32},{64... | collective-permute-start | bytes 6152 | tf_op jit(solution)/shard_map/while/body/eval_jaxpr/ppermute | solution.py:22
  323.9 19.2 %collective-permute-start.2 = (f32[2,256]{1,0:T(2,128)S(1)}, f32[2,256]{1,0:T(2,128)S(1)}, u32[]{:S(2)}, u32[]{:S(2)}) collective-permute-start(f32[2,256]{1,0:T(2,128)S(1)} %get-tuple-element.544), channel_id=1, source_target_pairs={{0,232},{8,240},{16,248},{24,0},{32,8},{40,16},{48,24},{56,32},{64... | collective-permute-start | bytes 6152 | tf_op jit(solution)/shard_map/while/body/eval_jaxpr/ppermute | solution.py:22
  372.9 15.0 %collective-permute-start.9 = (f32[2,256]{1,0:T(2,128)S(1)}, f32[2,256]{1,0:T(2,128)S(1)}, u32[]{:S(2)}, u32[]{:S(2)}) collective-permute-start(f32[2,256]{1,0:T(2,128)S(1)} %get-tuple-element.564), channel_id=1, source_target_pairs={{0,8},{8,16},{16,24},{24,32},{32,40},{40,48},{48,56},{56,64},{64,7... | collective-permute-start | bytes 6152 | tf_op jit(solution)/shard_map/while/body/eval_jaxpr/ppermute | solution.py:22
  373.0 20.9 %collective-permute-start.8 = (f32[2,256]{1,0:T(2,128)S(1)}, f32[2,256]{1,0:T(2,128)S(1)}, u32[]{:S(2)}, u32[]{:S(2)}) collective-permute-start(f32[2,256]{1,0:T(2,128)S(1)} %get-tuple-element.564), channel_id=1, source_target_pairs={{0,232},{8,240},{16,248},{24,0},{32,8},{40,16},{48,24},{56,32},{64... | collective-permute-start | bytes 6152 | tf_op jit(solution)/shard_map/while/body/eval_jaxpr/ppermute | solution.py:22
  380.5 13.5 %collective-permute-start.11 = (f32[2,256]{1,0:T(2,128)S(1)}, f32[2,256]{1,0:T(2,128)S(1)}, u32[]{:S(2)}, u32[]{:S(2)}) collective-permute-start(f32[2,256]{1,0:T(2,128)S(1)} %get-tuple-element.565), channel_id=1, source_target_pairs={{0,248},{8,0},{16,8},{24,16},{32,24},{40,32},{48,40},{56,48},{64,5... | collective-permute-start | bytes 6152 | tf_op jit(solution)/shard_map/while/body/eval_jaxpr/ppermute | solution.py:22
  423.3 14.6 %collective-permute-start.9 = (f32[2,256]{1,0:T(2,128)S(1)}, f32[2,256]{1,0:T(2,128)S(1)}, u32[]{:S(2)}, u32[]{:S(2)}) collective-permute-start(f32[2,256]{1,0:T(2,128)S(1)} %get-tuple-element.564), channel_id=1, source_target_pairs={{0,8},{8,16},{16,24},{24,32},{32,40},{40,48},{48,56},{56,64},{64,7... | collective-permute-start | bytes 6152 | tf_op jit(solution)/shard_map/while/body/eval_jaxpr/ppermute | solution.py:22
  423.3 20.7 %collective-permute-start.8 = (f32[2,256]{1,0:T(2,128)S(1)}, f32[2,256]{1,0:T(2,128)S(1)}, u32[]{:S(2)}, u32[]{:S(2)}) collective-permute-start(f32[2,256]{1,0:T(2,128)S(1)} %get-tuple-element.564), channel_id=1, source_target_pairs={{0,232},{8,240},{16,248},{24,0},{32,8},{40,16},{48,24},{56,32},{64... | collective-permute-start | bytes 6152 | tf_op jit(solution)/shard_map/while/body/eval_jaxpr/ppermute | solution.py:22
  430.5 13.5 %collective-permute-start.11 = (f32[2,256]{1,0:T(2,128)S(1)}, f32[2,256]{1,0:T(2,128)S(1)}, u32[]{:S(2)}, u32[]{:S(2)}) collective-permute-start(f32[2,256]{1,0:T(2,128)S(1)} %get-tuple-element.565), channel_id=1, source_target_pairs={{0,248},{8,0},{16,8},{24,16},{32,24},{40,32},{48,40},{56,48},{64,5... | collective-permute-start | bytes 6152 | tf_op jit(solution)/shard_map/while/body/eval_jaxpr/ppermute | solution.py:22
  473.3 14.1 %collective-permute-start.9 = (f32[2,256]{1,0:T(2,128)S(1)}, f32[2,256]{1,0:T(2,128)S(1)}, u32[]{:S(2)}, u32[]{:S(2)}) collective-permute-start(f32[2,256]{1,0:T(2,128)S(1)} %get-tuple-element.564), channel_id=1, source_target_pairs={{0,8},{8,16},{16,24},{24,32},{32,40},{40,48},{48,56},{56,64},{64,7... | collective-permute-start | bytes 6152 | tf_op jit(solution)/shard_map/while/body/eval_jaxpr/ppermute | solution.py:22
  473.3 20.2 %collective-permute-start.8 = (f32[2,256]{1,0:T(2,128)S(1)}, f32[2,256]{1,0:T(2,128)S(1)}, u32[]{:S(2)}, u32[]{:S(2)}) collective-permute-start(f32[2,256]{1,0:T(2,128)S(1)} %get-tuple-element.564), channel_id=1, source_target_pairs={{0,232},{8,240},{16,248},{24,0},{32,8},{40,16},{48,24},{56,32},{64... | collective-permute-start | bytes 6152 | tf_op jit(solution)/shard_map/while/body/eval_jaxpr/ppermute | solution.py:22
  480.1 13.4 %collective-permute-start.10 = (f32[2,256]{1,0:T(2,128)S(1)}, f32[2,256]{1,0:T(2,128)S(1)}, u32[]{:S(2)}, u32[]{:S(2)}) collective-permute-start(f32[2,256]{1,0:T(2,128)S(1)} %get-tuple-element.565), channel_id=1, source_target_pairs={{0,24},{8,32},{16,40},{24,48},{32,56},{40,64},{48,72},{56,80},{64,... | collective-permute-start | bytes 6152 | tf_op jit(solution)/shard_map/while/body/eval_jaxpr/ppermute | solution.py:22
  522.8 14.2 %collective-permute-start.9 = (f32[2,256]{1,0:T(2,128)S(1)}, f32[2,256]{1,0:T(2,128)S(1)}, u32[]{:S(2)}, u32[]{:S(2)}) collective-permute-start(f32[2,256]{1,0:T(2,128)S(1)} %get-tuple-element.564), channel_id=1, source_target_pairs={{0,8},{8,16},{16,24},{24,32},{32,40},{40,48},{48,56},{56,64},{64,7... | collective-permute-start | bytes 6152 | tf_op jit(solution)/shard_map/while/body/eval_jaxpr/ppermute | solution.py:22
  522.8 20.2 %collective-permute-start.8 = (f32[2,256]{1,0:T(2,128)S(1)}, f32[2,256]{1,0:T(2,128)S(1)}, u32[]{:S(2)}, u32[]{:S(2)}) collective-permute-start(f32[2,256]{1,0:T(2,128)S(1)} %get-tuple-element.564), channel_id=1, source_target_pairs={{0,232},{8,240},{16,248},{24,0},{32,8},{40,16},{48,24},{56,32},{64... | collective-permute-start | bytes 6152 | tf_op jit(solution)/shard_map/while/body/eval_jaxpr/ppermute | solution.py:22
  529.6 13.4 %collective-permute-start.10 = (f32[2,256]{1,0:T(2,128)S(1)}, f32[2,256]{1,0:T(2,128)S(1)}, u32[]{:S(2)}, u32[]{:S(2)}) collective-permute-start(f32[2,256]{1,0:T(2,128)S(1)} %get-tuple-element.565), channel_id=1, source_target_pairs={{0,24},{8,32},{16,40},{24,48},{32,56},{40,64},{48,72},{56,80},{64,... | collective-permute-start | bytes 6152 | tf_op jit(solution)/shard_map/while/body/eval_jaxpr/ppermute | solution.py:22
  572.3 14.2 %collective-permute-start.9 = (f32[2,256]{1,0:T(2,128)S(1)}, f32[2,256]{1,0:T(2,128)S(1)}, u32[]{:S(2)}, u32[]{:S(2)}) collective-permute-start(f32[2,256]{1,0:T(2,128)S(1)} %get-tuple-element.564), channel_id=1, source_target_pairs={{0,8},{8,16},{16,24},{24,32},{32,40},{40,48},{48,56},{56,64},{64,7... | collective-permute-start | bytes 6152 | tf_op jit(solution)/shard_map/while/body/eval_jaxpr/ppermute | solution.py:22
  572.3 20.2 %collective-permute-start.8 = (f32[2,256]{1,0:T(2,128)S(1)}, f32[2,256]{1,0:T(2,128)S(1)}, u32[]{:S(2)}, u32[]{:S(2)}) collective-permute-start(f32[2,256]{1,0:T(2,128)S(1)} %get-tuple-element.564), channel_id=1, source_target_pairs={{0,232},{8,240},{16,248},{24,0},{32,8},{40,16},{48,24},{56,32},{64... | collective-permute-start | bytes 6152 | tf_op jit(solution)/shard_map/while/body/eval_jaxpr/ppermute | solution.py:22
  579.2 13.4 %collective-permute-start.10 = (f32[2,256]{1,0:T(2,128)S(1)}, f32[2,256]{1,0:T(2,128)S(1)}, u32[]{:S(2)}, u32[]{:S(2)}) collective-permute-start(f32[2,256]{1,0:T(2,128)S(1)} %get-tuple-element.565), channel_id=1, source_target_pairs={{0,24},{8,32},{16,40},{24,48},{32,56},{40,64},{48,72},{56,80},{64,... | collective-permute-start | bytes 6152 | tf_op jit(solution)/shard_map/while/body/eval_jaxpr/ppermute | solution.py:22
  621.9 14.2 %collective-permute-start.9 = (f32[2,256]{1,0:T(2,128)S(1)}, f32[2,256]{1,0:T(2,128)S(1)}, u32[]{:S(2)}, u32[]{:S(2)}) collective-permute-start(f32[2,256]{1,0:T(2,128)S(1)} %get-tuple-element.564), channel_id=1, source_target_pairs={{0,8},{8,16},{16,24},{24,32},{32,40},{40,48},{48,56},{56,64},{64,7... | collective-permute-start | bytes 6152 | tf_op jit(solution)/shard_map/while/body/eval_jaxpr/ppermute | solution.py:22
  621.9 20.2 %collective-permute-start.8 = (f32[2,256]{1,0:T(2,128)S(1)}, f32[2,256]{1,0:T(2,128)S(1)}, u32[]{:S(2)}, u32[]{:S(2)}) collective-permute-start(f32[2,256]{1,0:T(2,128)S(1)} %get-tuple-element.564), channel_id=1, source_target_pairs={{0,232},{8,240},{16,248},{24,0},{32,8},{40,16},{48,24},{56,32},{64... | collective-permute-start | bytes 6152 | tf_op jit(solution)/shard_map/while/body/eval_jaxpr/ppermute | solution.py:22
  (117 other events, 927.4 us)
Sparse Core Ops, SparseCore 0:
  21.3 59.3 all-gather.1
where the time goes:
time: 797 us; the launch traced here: 788 us
  other arithmetic  349 us (44%)
  starting transfers between devices  189 us (24%)
  blocking collectives  100 us (13%)
  local copies, waits for them, and re-layouts  89.5 us (11%)
  waiting for transfers between devices  42.8 us (5%)
  between operations  15.9 us (2%)
    div x24, other arithmetic, face_flux(): -jnp.power(mean_depth, 5.0 / 3.0) * slope  185 us
    ppermute x26, starting transfers between devices, passed_along(): return lax.ppermute(block, axis, route)  95.5 us
    ppermute x52, starting transfers between devices, passed_along_2(): lax.ppermute(array, axis, [(i, (i + by) % devices) for i in range(devices)])  93.4 us
    psum x1, blocking collectives, local(): summed = lax.psum((misfit, cells), 'space')  72.3 us
    add x12, other arithmetic, advance(): level = padded + ground[None]  58.6 us
    add x12, other arithmetic, flow_step(): return ((ponded - intake) * land, soak_now + intake * land)  53.9 us
    slice x24, local copies, waits for them, and re-layouts, with_rims(): south = shift_rows(field[..., 0, :], -TX)  33.9 us
    psum x1, blocking collectives, local(): total = lax.psum(jnp.sum(raw), 'dom')  27.7 us
  transfers between devices with their start and end apart: 79, of which 14 were waited for; matrix products, arithmetic and copies ran while one was open for 12% of the time, Pallas kernels for 0%

commit v1 on v0

--- a/solution.py
+++ b/solution.py
@@ -111,7 +111,8 @@
     column_tile = lax.axis_index("space") % TX
     land = land_mask[0].astype(jnp.float32)
     ground = with_rims(terrain[0], column_tile)
-    window_forcing = lax.all_gather(forcing, "dom", axis=3, tiled=True)
+    stack = jnp.stack([forcing] * lax.axis_size("dom"))
+    window_forcing = jnp.concatenate(lax.all_to_all(stack, "dom", 0, 0), axis=3)
     misfit = jnp.zeros((per_group,), jnp.float32)
     for hour in range(HOURS):
         hour_forcing = window_forcing[hour]

time: 797 us -> 768 us (0.964)
  waiting for transfers between devices: 42.8 us -> 15.3 us
  between operations: 15.9 us -> 2.44 us
  starting transfers between devices: 189 us -> 198 us
    all_gather x1 -> x0, waiting for transfers between devices: 27.6 us -> none  [local(): window_forcing = lax.all_gather(forcing, 'dom', axis=3, tiled=True)]
    all_to_all x0 -> x1, starting transfers between devices: none -> 8.36 us  [local(): window_forcing = jnp.concatenate(lax.all_to_all(stack, 'dom', 0, 0), axis=3)]
  transfers between devices with their start and end apart: 79 -> 79, of which waited for: 14 -> 13; matrix products, arithmetic and copies ran while one was open for 12% -> 13% of each run, Pallas kernels for 0% -> 0%
where the time goes in v1:
time: 768 us; the launch traced here: 760 us
  other arithmetic  344 us (45%)
  starting transfers between devices  198 us (26%)
  blocking collectives  105 us (14%)
  local copies, waits for them, and re-layouts  92.7 us (12%)
  waiting for transfers between devices  15.3 us (2%)
    div x24, other arithmetic, face_flux(): -jnp.power(mean_depth, 5.0 / 3.0) * slope  185 us
    ppermute x26, starting transfers between devices, passed_along(): return lax.ppermute(block, axis, route)  95.5 us
    ppermute x52, starting transfers between devices, passed_along_2(): lax.ppermute(array, axis, [(i, (i + by) % devices) for i in range(devices)])  93.8 us
    psum x1, blocking collectives, local(): summed = lax.psum((misfit, cells), 'space')  72.8 us
    add x12, other arithmetic, advance(): level = padded + ground[None]  58.6 us
    add x12, other arithmetic, flow_step(): return ((ponded - intake) * land, soak_now + intake * land)  53.9 us
    slice x24, local copies, waits for them, and re-layouts, with_rims(): south = shift_rows(field[..., 0, :], -TX)  33.9 us
    psum x1, blocking collectives, local(): total = lax.psum(jnp.sum(raw), 'dom')  32.4 us
  transfers between devices with their start and end apart: 79, of which 13 were waited for; matrix products, arithmetic and copies ran while one was open for 13% of the time, Pallas kernels for 0%

profile of v1, /device:TPU:0, one launch (start us, length us, event | category | flops | bytes accessed | tf_op | source)
XLA Modules:
  0.0 759.8 jit_solution(466662421134141013)
XLA Ops:
  14.8 8.4 %all-to-all-start = ((bf16[8,2,2,1,32,512]{5,4,3,2,1,0:T(8,128)(2,1)}), bf16[8,2,2,1,32,512]{5,4,3,2,1,0:T(8,128)(2,1)}, u32[]{:S(2)}, u32[]{:S(2)}) async-start(bf16[8,2,2,1,32,512]{5,4,3,2,1,0:T(8,128)(2,1)} %stack.2), calls=%async_computation | async-start | bytes 2097152 | tf_op jit(solution)/shard_map/all_to_all | solution.py:115
  60.0 285.0 %while.28 = (s32[]{:T(128)}, f32[2,256,512]{1,0,2:T(2,128)S(1)}, f32[2,256,512]{1,0,2:T(2,128)}, pred[]{:T(512)}, pred[]{:T(512)}, /*index=5*/f32[258,514]{0,1:T...) while((s32[]{:T(128)}, f32[2,256,512]{1,0,2:T(2,128)S(1)}, ...), condition=%wide.region_4.6_spmd, body=%wide.region_3.5_spmd.sunk | while | flops 12489274 | bytes 36930208 | solution.py:129
  86.5 7.3 multiply_divide_fusion.4
  93.8 8.1 %fusion.45 = f32[2,257,512]{1,0,2:T(2,128)S(1)} fusion(f32[2,256,512]{1,0,2:T(2,128)S(1)} %get-tuple-element.607, f32[2,1,512]{1,0,2:T(2,128)S(1)} %copy.143, f32[2,1,512]{1,0,2:T(2,128)S(1)} %copy-done.5, f32[2,258,514]{1,0,2:T(2,128)S(1)} %maximum_add_fusion.6, f32[2]{0:T(128)S(1)} %bitcast.105), kind=kLoop, calls=%fused_computation.10.clone.1 | loop fusion | flops 2894848 | bytes 4214792 | tf_op jit(solution)/shard_map/while/body/eval_jaxpr/div | solution.py:61
  133.8 7.3 multiply_divide_fusion.4
  141.0 8.1 %fusion.45 = f32[2,257,512]{1,0,2:T(2,128)S(1)} fusion(f32[2,256,512]{1,0,2:T(2,128)S(1)} %get-tuple-element.607, f32[2,1,512]{1,0,2:T(2,128)S(1)} %copy.143, f32[2,1,512]{1,0,2:T(2,128)S(1)} %copy-done.5, f32[2,258,514]{1,0,2:T(2,128)S(1)} %maximum_add_fusion.6, f32[2]{0:T(128)S(1)} %bitcast.105), kind=kLoop, calls=%fused_computation.10.clone.1 | loop fusion | flops 2894848 | bytes 4214792 | tf_op jit(solution)/shard_map/while/body/eval_jaxpr/div | solution.py:61
  181.0 7.3 multiply_divide_fusion.4
  188.3 8.1 %fusion.45 = f32[2,257,512]{1,0,2:T(2,128)S(1)} fusion(f32[2,256,512]{1,0,2:T(2,128)S(1)} %get-tuple-element.607, f32[2,1,512]{1,0,2:T(2,128)S(1)} %copy.143, f32[2,1,512]{1,0,2:T(2,128)S(1)} %copy-done.5, f32[2,258,514]{1,0,2:T(2,128)S(1)} %maximum_add_fusion.6, f32[2]{0:T(128)S(1)} %bitcast.105), kind=kLoop, calls=%fused_computation.10.clone.1 | loop fusion | flops 2894848 | bytes 4214792 | tf_op jit(solution)/shard_map/while/body/eval_jaxpr/div | solution.py:61
  228.2 7.3 multiply_divide_fusion.4
  235.5 8.1 %fusion.45 = f32[2,257,512]{1,0,2:T(2,128)S(1)} fusion(f32[2,256,512]{1,0,2:T(2,128)S(1)} %get-tuple-element.607, f32[2,1,512]{1,0,2:T(2,128)S(1)} %copy.143, f32[2,1,512]{1,0,2:T(2,128)S(1)} %copy-done.5, f32[2,258,514]{1,0,2:T(2,128)S(1)} %maximum_add_fusion.6, f32[2]{0:T(128)S(1)} %bitcast.105), kind=kLoop, calls=%fused_computation.10.clone.1 | loop fusion | flops 2894848 | bytes 4214792 | tf_op jit(solution)/shard_map/while/body/eval_jaxpr/div | solution.py:61
  275.5 7.3 multiply_divide_fusion.4
  282.7 8.1 %fusion.45 = f32[2,257,512]{1,0,2:T(2,128)S(1)} fusion(f32[2,256,512]{1,0,2:T(2,128)S(1)} %get-tuple-element.607, f32[2,1,512]{1,0,2:T(2,128)S(1)} %copy.143, f32[2,1,512]{1,0,2:T(2,128)S(1)} %copy-done.5, f32[2,258,514]{1,0,2:T(2,128)S(1)} %maximum_add_fusion.6, f32[2]{0:T(128)S(1)} %bitcast.105), kind=kLoop, calls=%fused_computation.10.clone.1 | loop fusion | flops 2894848 | bytes 4214792 | tf_op jit(solution)/shard_map/while/body/eval_jaxpr/div | solution.py:61
  296.4 7.8 %collective-permute-start.2 = (f32[2,256]{1,0:T(2,128)S(1)}, f32[2,256]{1,0:T(2,128)S(1)}, u32[]{:S(2)}, u32[]{:S(2)}) collective-permute-start(f32[2,256]{1,0:T(2,128)S(1)} %get-tuple-element.566), channel_id=1, source_target_pairs={{0,232},{8,240},{16,248},{24,0},{32,8},{40,16},{48,24},{56,32},{64... | collective-permute-start | bytes 6152 | tf_op jit(solution)/shard_map/while/body/eval_jaxpr/ppermute | solution.py:22
  323.9 7.3 multiply_divide_fusion.4
  331.2 8.1 %fusion.45 = f32[2,257,512]{1,0,2:T(2,128)S(1)} fusion(f32[2,256,512]{1,0,2:T(2,128)S(1)} %get-tuple-element.607, f32[2,1,512]{1,0,2:T(2,128)S(1)} %copy.143, f32[2,1,512]{1,0,2:T(2,128)S(1)} %copy-done.5, f32[2,258,514]{1,0,2:T(2,128)S(1)} %maximum_add_fusion.6, f32[2]{0:T(128)S(1)} %bitcast.105), kind=kLoop, calls=%fused_computation.10.clone.1 | loop fusion | flops 2894848 | bytes 4214792 | tf_op jit(solution)/shard_map/while/body/eval_jaxpr/div | solution.py:61
  346.2 298.3 %while.29 = (s32[]{:T(128)}, f32[2,256,512]{1,0,2:T(2,128)S(1)}, f32[2,256,512]{1,0,2:T(2,128)}, pred[]{:T(512)}, pred[]{:T(512)}, /*index=5*/f32[258,514]{0,1:T...) while((s32[]{:T(128)}, f32[2,256,512]{1,0,2:T(2,128)S(1)}, ...), condition=%wide.region_6.8_spmd, body=%wide.region_5.7_spmd.sunk | while | flops 12489274 | bytes 39043804 | solution.py:129
  346.3 7.5 collective-permute-start.8
  375.6 7.3 multiply_divide_fusion.5
  382.9 8.1 %fusion.48 = f32[2,257,512]{1,0,2:T(2,128)S(1)} fusion(f32[2,256,512]{1,0,2:T(2,128)S(1)} %get-tuple-element.646, f32[2,1,512]{1,0,2:T(2,128)S(1)} %copy-done.4, f32[2,1,512]{1,0,2:T(2,128)S(1)} %copy-done.6, f32[2,258,514]{1,0,2:T(2,128)S(1)} %maximum_add_fusion.7, f32[2]{0:T(128)S(1)} %bitcast.107), kind=kLoop, calls=%fused_computation.50.clone.1 | loop fusion | flops 2894848 | bytes 4214792 | tf_op jit(solution)/shard_map/while/body/eval_jaxpr/div | solution.py:61
  425.2 7.3 multiply_divide_fusion.5
  432.5 8.1 %fusion.48 = f32[2,257,512]{1,0,2:T(2,128)S(1)} fusion(f32[2,256,512]{1,0,2:T(2,128)S(1)} %get-tuple-element.646, f32[2,1,512]{1,0,2:T(2,128)S(1)} %copy-done.4, f32[2,1,512]{1,0,2:T(2,128)S(1)} %copy-done.6, f32[2,258,514]{1,0,2:T(2,128)S(1)} %maximum_add_fusion.7, f32[2]{0:T(128)S(1)} %bitcast.107), kind=kLoop, calls=%fused_computation.50.clone.1 | loop fusion | flops 2894848 | bytes 4214792 | tf_op jit(solution)/shard_map/while/body/eval_jaxpr/div | solution.py:61
  446.1 6.9 collective-permute-start.8
  474.8 7.3 multiply_divide_fusion.5
  482.1 8.1 %fusion.48 = f32[2,257,512]{1,0,2:T(2,128)S(1)} fusion(f32[2,256,512]{1,0,2:T(2,128)S(1)} %get-tuple-element.646, f32[2,1,512]{1,0,2:T(2,128)S(1)} %copy-done.4, f32[2,1,512]{1,0,2:T(2,128)S(1)} %copy-done.6, f32[2,258,514]{1,0,2:T(2,128)S(1)} %maximum_add_fusion.7, f32[2]{0:T(128)S(1)} %bitcast.107), kind=kLoop, calls=%fused_computation.50.clone.1 | loop fusion | flops 2894848 | bytes 4214792 | tf_op jit(solution)/shard_map/while/body/eval_jaxpr/div | solution.py:61
  524.3 7.3 multiply_divide_fusion.5
  531.6 8.1 %fusion.48 = f32[2,257,512]{1,0,2:T(2,128)S(1)} fusion(f32[2,256,512]{1,0,2:T(2,128)S(1)} %get-tuple-element.646, f32[2,1,512]{1,0,2:T(2,128)S(1)} %copy-done.4, f32[2,1,512]{1,0,2:T(2,128)S(1)} %copy-done.6, f32[2,258,514]{1,0,2:T(2,128)S(1)} %maximum_add_fusion.7, f32[2]{0:T(128)S(1)} %bitcast.107), kind=kLoop, calls=%fused_computation.50.clone.1 | loop fusion | flops 2894848 | bytes 4214792 | tf_op jit(solution)/shard_map/while/body/eval_jaxpr/div | solution.py:61
  573.9 7.3 multiply_divide_fusion.5
  581.2 8.1 %fusion.48 = f32[2,257,512]{1,0,2:T(2,128)S(1)} fusion(f32[2,256,512]{1,0,2:T(2,128)S(1)} %get-tuple-element.646, f32[2,1,512]{1,0,2:T(2,128)S(1)} %copy-done.4, f32[2,1,512]{1,0,2:T(2,128)S(1)} %copy-done.6, f32[2,258,514]{1,0,2:T(2,128)S(1)} %maximum_add_fusion.7, f32[2]{0:T(128)S(1)} %bitcast.107), kind=kLoop, calls=%fused_computation.50.clone.1 | loop fusion | flops 2894848 | bytes 4214792 | tf_op jit(solution)/shard_map/while/body/eval_jaxpr/div | solution.py:61
  623.5 7.3 multiply_divide_fusion.5
  630.8 8.1 %fusion.48 = f32[2,257,512]{1,0,2:T(2,128)S(1)} fusion(f32[2,256,512]{1,0,2:T(2,128)S(1)} %get-tuple-element.646, f32[2,1,512]{1,0,2:T(2,128)S(1)} %copy-done.4, f32[2,1,512]{1,0,2:T(2,128)S(1)} %copy-done.6, f32[2,258,514]{1,0,2:T(2,128)S(1)} %maximum_add_fusion.7, f32[2]{0:T(128)S(1)} %bitcast.107), kind=kLoop, calls=%fused_computation.50.clone.1 | loop fusion | flops 2894848 | bytes 4214792 | tf_op jit(solution)/shard_map/while/body/eval_jaxpr/div | solution.py:61
  651.8 72.8 %all-reduce = (f32[2]{0:T(128)S(1)}, f32[]{:T(128)}) all-reduce(f32[2]{0:T(128)S(1)} %add.160, f32[]{:T(128)S(6)} %mul.249), channel_id=1, replica_groups=mesh['space'=32,'dom'=8] {'space'}, use_global_device_ids=true, to_apply=%region_10.12 | all-reduce | flops 3 | bytes 24 | tf_op jit(solution)/shard_map/psum | solution.py:134
  725.9 32.4 %psum.23 = f32[]{:T(128)} all-reduce(f32[]{:T(128)} %get-tuple-element.397), channel_id=1, replica_groups=mesh['space'=32,'dom'=8] {'dom'}, use_global_device_ids=true, to_apply=%region_14.16 | all-reduce | flops 1 | bytes 8 | tf_op jit(solution)/shard_map/psum | solution.py:136
  (505 shorter events, 434.6 us)
Async XLA Ops:
  2.0 42.1 %collective-permute-start.17 = (f32[256]{0:T(256)S(1)}, f32[256]{0:T(256)S(1)}, u32[]{:S(2)}, u32[]{:S(2)}) collective-permute-start(f32[256]{0:T(256)S(1)} %bitcast.129), channel_id=1, source_target_pairs={{0,248},{8,0},{16,8},{24,16},{32,24},{40,32},{48,40},{56,48},{64,5... | collective-permute-start | bytes 3080 | tf_op jit(solution)/shard_map/ppermute | solution.py:22
  6.9 43.3 %collective-permute-start.16 = (f32[256]{0:T(256)S(1)}, f32[256]{0:T(256)S(1)}, u32[]{:S(2)}, u32[]{:S(2)}) collective-permute-start(f32[256]{0:T(256)S(1)} %bitcast.130), channel_id=1, source_target_pairs={{0,24},{8,32},{16,40},{24,48},{32,56},{40,64},{48,72},{56,80},{64,... | collective-permute-start | bytes 3080 | tf_op jit(solution)/shard_map/ppermute | solution.py:22
  6.9 43.4 %collective-permute-start.13 = (f32[256]{0:T(256)S(1)}, f32[256]{0:T(256)S(1)}, u32[]{:S(2)}, u32[]{:S(2)}) collective-permute-start(f32[256]{0:T(256)S(1)} %bitcast.127), channel_id=1, source_target_pairs={{0,8},{8,16},{16,24},{24,32},{32,40},{40,48},{48,56},{56,64},{64,7... | collective-permute-start | bytes 3080 | tf_op jit(solution)/shard_map/ppermute | solution.py:22
  6.9 43.4 %collective-permute-start.12 = (f32[256]{0:T(256)S(1)}, f32[256]{0:T(256)S(1)}, u32[]{:S(2)}, u32[]{:S(2)}) collective-permute-start(f32[256]{0:T(256)S(1)} %bitcast.128), channel_id=1, source_target_pairs={{0,232},{8,240},{16,248},{24,0},{32,8},{40,16},{48,24},{56,32},{64... | collective-permute-start | bytes 3080 | tf_op jit(solution)/shard_map/ppermute | solution.py:22
  14.8 39.8 %all-to-all-start = ((bf16[8,2,2,1,32,512]{5,4,3,2,1,0:T(8,128)(2,1)}), bf16[8,2,2,1,32,512]{5,4,3,2,1,0:T(8,128)(2,1)}, u32[]{:S(2)}, u32[]{:S(2)}) async-start(bf16[8,2,2,1,32,512]{5,4,3,2,1,0:T(8,128)(2,1)} %stack.2), calls=%async_computation | async-start | bytes 2097152 | tf_op jit(solution)/shard_map/all_to_all | solution.py:115
  60.2 18.8 %collective-permute-start.2 = (f32[2,256]{1,0:T(2,128)S(1)}, f32[2,256]{1,0:T(2,128)S(1)}, u32[]{:S(2)}, u32[]{:S(2)}) collective-permute-start(f32[2,256]{1,0:T(2,128)S(1)} %get-tuple-element.566), channel_id=1, source_target_pairs={{0,232},{8,240},{16,248},{24,0},{32,8},{40,16},{48,24},{56,32},{64... | collective-permute-start | bytes 6152 | tf_op jit(solution)/shard_map/while/body/eval_jaxpr/ppermute | solution.py:22
  63.5 15.5 %collective-permute-start.5 = (f32[2,256]{1,0:T(2,128)S(1)}, f32[2,256]{1,0:T(2,128)S(1)}, u32[]{:S(2)}, u32[]{:S(2)}) collective-permute-start(f32[2,256]{1,0:T(2,128)S(1)} %get-tuple-element.567), channel_id=1, source_target_pairs={{0,248},{8,0},{16,8},{24,16},{32,24},{40,32},{48,40},{56,48},{64,5... | collective-permute-start | bytes 6152 | tf_op jit(solution)/shard_map/while/body/eval_jaxpr/ppermute | solution.py:22
  107.5 18.8 %collective-permute-start.2 = (f32[2,256]{1,0:T(2,128)S(1)}, f32[2,256]{1,0:T(2,128)S(1)}, u32[]{:S(2)}, u32[]{:S(2)}) collective-permute-start(f32[2,256]{1,0:T(2,128)S(1)} %get-tuple-element.566), channel_id=1, source_target_pairs={{0,232},{8,240},{16,248},{24,0},{32,8},{40,16},{48,24},{56,32},{64... | collective-permute-start | bytes 6152 | tf_op jit(solution)/shard_map/while/body/eval_jaxpr/ppermute | solution.py:22
  111.0 15.3 %collective-permute-start.5 = (f32[2,256]{1,0:T(2,128)S(1)}, f32[2,256]{1,0:T(2,128)S(1)}, u32[]{:S(2)}, u32[]{:S(2)}) collective-permute-start(f32[2,256]{1,0:T(2,128)S(1)} %get-tuple-element.567), channel_id=1, source_target_pairs={{0,248},{8,0},{16,8},{24,16},{32,24},{40,32},{48,40},{56,48},{64,5... | collective-permute-start | bytes 6152 | tf_op jit(solution)/shard_map/while/body/eval_jaxpr/ppermute | solution.py:22
  154.7 18.8 %collective-permute-start.2 = (f32[2,256]{1,0:T(2,128)S(1)}, f32[2,256]{1,0:T(2,128)S(1)}, u32[]{:S(2)}, u32[]{:S(2)}) collective-permute-start(f32[2,256]{1,0:T(2,128)S(1)} %get-tuple-element.566), channel_id=1, source_target_pairs={{0,232},{8,240},{16,248},{24,0},{32,8},{40,16},{48,24},{56,32},{64... | collective-permute-start | bytes 6152 | tf_op jit(solution)/shard_map/while/body/eval_jaxpr/ppermute | solution.py:22
  158.9 14.7 %collective-permute-start.5 = (f32[2,256]{1,0:T(2,128)S(1)}, f32[2,256]{1,0:T(2,128)S(1)}, u32[]{:S(2)}, u32[]{:S(2)}) collective-permute-start(f32[2,256]{1,0:T(2,128)S(1)} %get-tuple-element.567), channel_id=1, source_target_pairs={{0,248},{8,0},{16,8},{24,16},{32,24},{40,32},{48,40},{56,48},{64,5... | collective-permute-start | bytes 6152 | tf_op jit(solution)/shard_map/while/body/eval_jaxpr/ppermute | solution.py:22
  201.9 18.8 %collective-permute-start.2 = (f32[2,256]{1,0:T(2,128)S(1)}, f32[2,256]{1,0:T(2,128)S(1)}, u32[]{:S(2)}, u32[]{:S(2)}) collective-permute-start(f32[2,256]{1,0:T(2,128)S(1)} %get-tuple-element.566), channel_id=1, source_target_pairs={{0,232},{8,240},{16,248},{24,0},{32,8},{40,16},{48,24},{56,32},{64... | collective-permute-start | bytes 6152 | tf_op jit(solution)/shard_map/while/body/eval_jaxpr/ppermute | solution.py:22
  206.5 14.3 %collective-permute-start.5 = (f32[2,256]{1,0:T(2,128)S(1)}, f32[2,256]{1,0:T(2,128)S(1)}, u32[]{:S(2)}, u32[]{:S(2)}) collective-permute-start(f32[2,256]{1,0:T(2,128)S(1)} %get-tuple-element.567), channel_id=1, source_target_pairs={{0,248},{8,0},{16,8},{24,16},{32,24},{40,32},{48,40},{56,48},{64,5... | collective-permute-start | bytes 6152 | tf_op jit(solution)/shard_map/while/body/eval_jaxpr/ppermute | solution.py:22
  249.2 18.8 %collective-permute-start.2 = (f32[2,256]{1,0:T(2,128)S(1)}, f32[2,256]{1,0:T(2,128)S(1)}, u32[]{:S(2)}, u32[]{:S(2)}) collective-permute-start(f32[2,256]{1,0:T(2,128)S(1)} %get-tuple-element.566), channel_id=1, source_target_pairs={{0,232},{8,240},{16,248},{24,0},{32,8},{40,16},{48,24},{56,32},{64... | collective-permute-start | bytes 6152 | tf_op jit(solution)/shard_map/while/body/eval_jaxpr/ppermute | solution.py:22
  296.4 14.0 %collective-permute-start.3 = (f32[2,256]{1,0:T(2,128)S(1)}, f32[2,256]{1,0:T(2,128)S(1)}, u32[]{:S(2)}, u32[]{:S(2)}) collective-permute-start(f32[2,256]{1,0:T(2,128)S(1)} %get-tuple-element.566), channel_id=1, source_target_pairs={{0,8},{8,16},{16,24},{24,32},{32,40},{40,48},{48,56},{56,64},{64,7... | collective-permute-start | bytes 6152 | tf_op jit(solution)/shard_map/while/body/eval_jaxpr/ppermute | solution.py:22
  296.4 20.0 %collective-permute-start.2 = (f32[2,256]{1,0:T(2,128)S(1)}, f32[2,256]{1,0:T(2,128)S(1)}, u32[]{:S(2)}, u32[]{:S(2)}) collective-permute-start(f32[2,256]{1,0:T(2,128)S(1)} %get-tuple-element.566), channel_id=1, source_target_pairs={{0,232},{8,240},{16,248},{24,0},{32,8},{40,16},{48,24},{56,32},{64... | collective-permute-start | bytes 6152 | tf_op jit(solution)/shard_map/while/body/eval_jaxpr/ppermute | solution.py:22
  346.2 15.0 %collective-permute-start.9 = (f32[2,256]{1,0:T(2,128)S(1)}, f32[2,256]{1,0:T(2,128)S(1)}, u32[]{:S(2)}, u32[]{:S(2)}) collective-permute-start(f32[2,256]{1,0:T(2,128)S(1)} %get-tuple-element.586), channel_id=1, source_target_pairs={{0,8},{8,16},{16,24},{24,32},{32,40},{40,48},{48,56},{56,64},{64,7... | collective-permute-start | bytes 6152 | tf_op jit(solution)/shard_map/while/body/eval_jaxpr/ppermute | solution.py:22
  346.3 20.9 %collective-permute-start.8 = (f32[2,256]{1,0:T(2,128)S(1)}, f32[2,256]{1,0:T(2,128)S(1)}, u32[]{:S(2)}, u32[]{:S(2)}) collective-permute-start(f32[2,256]{1,0:T(2,128)S(1)} %get-tuple-element.586), channel_id=1, source_target_pairs={{0,232},{8,240},{16,248},{24,0},{32,8},{40,16},{48,24},{56,32},{64... | collective-permute-start | bytes 6152 | tf_op jit(solution)/shard_map/while/body/eval_jaxpr/ppermute | solution.py:22
  353.8 13.5 %collective-permute-start.11 = (f32[2,256]{1,0:T(2,128)S(1)}, f32[2,256]{1,0:T(2,128)S(1)}, u32[]{:S(2)}, u32[]{:S(2)}) collective-permute-start(f32[2,256]{1,0:T(2,128)S(1)} %get-tuple-element.587), channel_id=1, source_target_pairs={{0,248},{8,0},{16,8},{24,16},{32,24},{40,32},{48,40},{56,48},{64,5... | collective-permute-start | bytes 6152 | tf_op jit(solution)/shard_map/while/body/eval_jaxpr/ppermute | solution.py:22
  396.6 14.1 %collective-permute-start.9 = (f32[2,256]{1,0:T(2,128)S(1)}, f32[2,256]{1,0:T(2,128)S(1)}, u32[]{:S(2)}, u32[]{:S(2)}) collective-permute-start(f32[2,256]{1,0:T(2,128)S(1)} %get-tuple-element.586), channel_id=1, source_target_pairs={{0,8},{8,16},{16,24},{24,32},{32,40},{40,48},{48,56},{56,64},{64,7... | collective-permute-start | bytes 6152 | tf_op jit(solution)/shard_map/while/body/eval_jaxpr/ppermute | solution.py:22
  396.6 20.2 %collective-permute-start.8 = (f32[2,256]{1,0:T(2,128)S(1)}, f32[2,256]{1,0:T(2,128)S(1)}, u32[]{:S(2)}, u32[]{:S(2)}) collective-permute-start(f32[2,256]{1,0:T(2,128)S(1)} %get-tuple-element.586), channel_id=1, source_target_pairs={{0,232},{8,240},{16,248},{24,0},{32,8},{40,16},{48,24},{56,32},{64... | collective-permute-start | bytes 6152 | tf_op jit(solution)/shard_map/while/body/eval_jaxpr/ppermute | solution.py:22
  403.4 13.4 %collective-permute-start.10 = (f32[2,256]{1,0:T(2,128)S(1)}, f32[2,256]{1,0:T(2,128)S(1)}, u32[]{:S(2)}, u32[]{:S(2)}) collective-permute-start(f32[2,256]{1,0:T(2,128)S(1)} %get-tuple-element.587), channel_id=1, source_target_pairs={{0,24},{8,32},{16,40},{24,48},{32,56},{40,64},{48,72},{56,80},{64,... | collective-permute-start | bytes 6152 | tf_op jit(solution)/shard_map/while/body/eval_jaxpr/ppermute | solution.py:22
  446.1 14.2 %collective-permute-start.9 = (f32[2,256]{1,0:T(2,128)S(1)}, f32[2,256]{1,0:T(2,128)S(1)}, u32[]{:S(2)}, u32[]{:S(2)}) collective-permute-start(f32[2,256]{1,0:T(2,128)S(1)} %get-tuple-element.586), channel_id=1, source_target_pairs={{0,8},{8,16},{16,24},{24,32},{32,40},{40,48},{48,56},{56,64},{64,7... | collective-permute-start | bytes 6152 | tf_op jit(solution)/shard_map/while/body/eval_jaxpr/ppermute | solution.py:22
  446.1 20.2 %collective-permute-start.8 = (f32[2,256]{1,0:T(2,128)S(1)}, f32[2,256]{1,0:T(2,128)S(1)}, u32[]{:S(2)}, u32[]{:S(2)}) collective-permute-start(f32[2,256]{1,0:T(2,128)S(1)} %get-tuple-element.586), channel_id=1, source_target_pairs={{0,232},{8,240},{16,248},{24,0},{32,8},{40,16},{48,24},{56,32},{64... | collective-permute-start | bytes 6152 | tf_op jit(solution)/shard_map/while/body/eval_jaxpr/ppermute | solution.py:22
  453.0 13.4 %collective-permute-start.10 = (f32[2,256]{1,0:T(2,128)S(1)}, f32[2,256]{1,0:T(2,128)S(1)}, u32[]{:S(2)}, u32[]{:S(2)}) collective-permute-start(f32[2,256]{1,0:T(2,128)S(1)} %get-tuple-element.587), channel_id=1, source_target_pairs={{0,24},{8,32},{16,40},{24,48},{32,56},{40,64},{48,72},{56,80},{64,... | collective-permute-start | bytes 6152 | tf_op jit(solution)/shard_map/while/body/eval_jaxpr/ppermute | solution.py:22
  495.7 14.2 %collective-permute-start.9 = (f32[2,256]{1,0:T(2,128)S(1)}, f32[2,256]{1,0:T(2,128)S(1)}, u32[]{:S(2)}, u32[]{:S(2)}) collective-permute-start(f32[2,256]{1,0:T(2,128)S(1)} %get-tuple-element.586), channel_id=1, source_target_pairs={{0,8},{8,16},{16,24},{24,32},{32,40},{40,48},{48,56},{56,64},{64,7... | collective-permute-start | bytes 6152 | tf_op jit(solution)/shard_map/while/body/eval_jaxpr/ppermute | solution.py:22
  495.7 20.2 %collective-permute-start.8 = (f32[2,256]{1,0:T(2,128)S(1)}, f32[2,256]{1,0:T(2,128)S(1)}, u32[]{:S(2)}, u32[]{:S(2)}) collective-permute-start(f32[2,256]{1,0:T(2,128)S(1)} %get-tuple-element.586), channel_id=1, source_target_pairs={{0,232},{8,240},{16,248},{24,0},{32,8},{40,16},{48,24},{56,32},{64... | collective-permute-start | bytes 6152 | tf_op jit(solution)/shard_map/while/body/eval_jaxpr/ppermute | solution.py:22
  502.6 13.4 %collective-permute-start.10 = (f32[2,256]{1,0:T(2,128)S(1)}, f32[2,256]{1,0:T(2,128)S(1)}, u32[]{:S(2)}, u32[]{:S(2)}) collective-permute-start(f32[2,256]{1,0:T(2,128)S(1)} %get-tuple-element.587), channel_id=1, source_target_pairs={{0,24},{8,32},{16,40},{24,48},{32,56},{40,64},{48,72},{56,80},{64,... | collective-permute-start | bytes 6152 | tf_op jit(solution)/shard_map/while/body/eval_jaxpr/ppermute | solution.py:22
  545.3 14.2 %collective-permute-start.9 = (f32[2,256]{1,0:T(2,128)S(1)}, f32[2,256]{1,0:T(2,128)S(1)}, u32[]{:S(2)}, u32[]{:S(2)}) collective-permute-start(f32[2,256]{1,0:T(2,128)S(1)} %get-tuple-element.586), channel_id=1, source_target_pairs={{0,8},{8,16},{16,24},{24,32},{32,40},{40,48},{48,56},{56,64},{64,7... | collective-permute-start | bytes 6152 | tf_op jit(solution)/shard_map/while/body/eval_jaxpr/ppermute | solution.py:22
  545.3 20.2 %collective-permute-start.8 = (f32[2,256]{1,0:T(2,128)S(1)}, f32[2,256]{1,0:T(2,128)S(1)}, u32[]{:S(2)}, u32[]{:S(2)}) collective-permute-start(f32[2,256]{1,0:T(2,128)S(1)} %get-tuple-element.586), channel_id=1, source_target_pairs={{0,232},{8,240},{16,248},{24,0},{32,8},{40,16},{48,24},{56,32},{64... | collective-permute-start | bytes 6152 | tf_op jit(solution)/shard_map/while/body/eval_jaxpr/ppermute | solution.py:22
  594.9 14.2 %collective-permute-start.9 = (f32[2,256]{1,0:T(2,128)S(1)}, f32[2,256]{1,0:T(2,128)S(1)}, u32[]{:S(2)}, u32[]{:S(2)}) collective-permute-start(f32[2,256]{1,0:T(2,128)S(1)} %get-tuple-element.586), channel_id=1, source_target_pairs={{0,8},{8,16},{16,24},{24,32},{32,40},{40,48},{48,56},{56,64},{64,7... | collective-permute-start | bytes 6152 | tf_op jit(solution)/shard_map/while/body/eval_jaxpr/ppermute | solution.py:22
  594.9 20.2 %collective-permute-start.8 = (f32[2,256]{1,0:T(2,128)S(1)}, f32[2,256]{1,0:T(2,128)S(1)}, u32[]{:S(2)}, u32[]{:S(2)}) collective-permute-start(f32[2,256]{1,0:T(2,128)S(1)} %get-tuple-element.586), channel_id=1, source_target_pairs={{0,232},{8,240},{16,248},{24,0},{32,8},{40,16},{48,24},{56,32},{64... | collective-permute-start | bytes 6152 | tf_op jit(solution)/shard_map/while/body/eval_jaxpr/ppermute | solution.py:22
  (118 other events, 941.3 us)
